TPU v7x, 128 devices: a whole 4x4x4 slice. The times are simulated.
128 devices in a mesh: grp: 2 (over y_lo), orb: 64 (over y_hi, z, x, core).
Axes of the slice: x: 4, y: 4 (y_hi: 2, y_lo: 2; y = y_hi * 2 + y_lo), z: 4, core: 2. Of those that a mesh axis runs over, the one named last changes fastest.
Arguments:
- occupied: float32 [64, 262144], P('orb'), may hold values from -5 to 5
- targets: float32 [128, 262144], P(('grp', 'orb')), may hold values from -8 to 8
- potential: float32 [262144], P('orb'), may hold values from -4 to 4
Outputs:
- updated: float32 [128, 262144], P('grp', 'orb')
All inputs are finite; a program needn't handle non-finite values.
Results may differ from a plain program's by a relative error of at most 0.0003.
Values sent between devices are 32-bit elements; how exact they have to be, the bound alone decides.
A program may use at most 64 MiB of HBM per device.

v0:
```python
import functools
import ml_dtypes
import jax
import jax.numpy as jnp
from jax.sharding import PartitionSpec as P
from jax import lax
from jax.experimental import pallas as pl
from jax.experimental.pallas import tpu as pltpu
import numpy as np
BF=jnp.bfloat16; F32=jnp.float32
MESH=pl.DeviceIdType.MESH
CELLS=262144
NDEV=128
CH=4
CP=32//CH
CR=2048//CH

def tables():
    bf=ml_dtypes.bfloat16
    i=np.arange(64)
    ang=2*np.pi*((i[:,None]*i[None,:])%64)/64
    H=(np.cos(ang)+np.sin(ang)).astype(np.float32)
    Hh=H.astype(bf); Hl=(H-Hh.astype(np.float32)).astype(bf)
    perm=2*(i%32)+i//32
    ax=np.concatenate([Hh,Hh,Hl],1)
    ay=ax.reshape(64,3,64)[perm][:,:,perm].reshape(64,192)
    z=np.zeros((64,64),bf)
    bd=lambda m: np.block([[m,z],[z,m]])
    row=np.concatenate([bd(Hh),bd(Hl)],1)
    wz=np.concatenate([row,row],0)
    q=np.minimum(i,64-i).astype(np.float32)*np.float32(2*np.pi/20.0); q2=q*q
    qa=np.broadcast_to((q2+np.float32(0.04))[:,None],(64,128))
    qb=q2.reshape(32,2)
    qr=(qb[:,:,None]+q2[None,None,:]).reshape(32,128)
    return ax,ay,wz,np.concatenate([qa,qr],0).astype(np.float32)

def split(x):
    h=x.astype(BF)
    return h,(x-h.astype(F32)).astype(BF)
def dot(a,b): return jnp.dot(a,b,preferred_element_type=F32)
def half_swap(lo,hi,mask):
    return jnp.where(mask,lo,pltpu.roll(hi,64,1)), jnp.where(mask,pltpu.roll(lo,64,1),hi)
def left(A,planes):
    out=[]
    for k in range(0,len(planes),2):
        h,l=split(jnp.concatenate(planes[k:k+2],1))
        r=dot(A,jnp.concatenate([h,l,h],0))
        out+=[r[:,:128],r[:,128:]]
    return out
def lanes(x,W):
    h,l=split(x)
    r=dot(jnp.concatenate([h,l],1),W)
    return r[:,:128]+r[:,128:]

def peer(d): return (d//64,lax.rem(d,64))

def k1(t_ref,o_ref,ax_ref,ay_ref,wz_ref,q_ref,tc,ec,ob,sb,kt,e,osend,arecv,brecv,crecv,drecv,tsend,trecv,esend,erecv,loc):
    g=lax.axis_index("grp"); o=lax.axis_index("orb"); me=g*64+o
    s=2*lax.rem(o,2)-1
    w=lambda v: lax.rem(v+128,64)
    inner=(g,w(o-s)); outer=(g,w(o+s)); across=(g,w(o-2*s))
    bar=pltpu.get_barrier_semaphore()
    def sig(k,c):
        pl.semaphore_signal(bar,inc=1,device_id=peer(lax.rem(me+k,NDEV)),device_id_type=MESH)
        return c
    lax.fori_loop(1,NDEV,sig,0)
    own=pltpu.make_async_copy(o_ref,ob.at[0],loc); own.start()
    mask=lax.broadcasted_iota(jnp.int32,(32,128),1)<64
    ax=ax_ref[...];ay=ay_ref[...];wz=wz_ref[...]
    qa=q_ref[0:64,:]
    def ktab(r,c):
        kt[pl.ds(pl.multiple_of(r*64,64),64),:]=(4*np.pi/CELLS)/(qa+q_ref[pl.ds(64+r,1),:])
        return c
    lax.fori_loop(0,32,ktab,0,unroll=8)
    own.wait()
    def rows(q): return pl.ds(pl.multiple_of(q*CR,CR),CR)
    def fwd(j,q):
        pr=t_ref[rows(q),:]*ob[j,rows(q),:]
        b=[]
        for p in range(CP):
            b+=half_swap(pr[64*p:64*p+32],pr[64*p+32:64*p+64],mask)
        x=lanes(jnp.concatenate(b,0),wz)
        f=left(ay,[x[64*p:64*p+64] for p in range(CP)])
        out=[]
        for p in range(CP): out+=half_swap(f[p][:32],f[p][32:],mask)
        sb[j,rows(q),:]=jnp.concatenate(out,0)
    R=16
    def mid(j):
        def half(i,c):
            f=left(ax,[sb[j,pl.ds(i*R+r,64,stride=32),:] for r in range(R)])
            kk=kt[pl.ds(pl.multiple_of(i*R*64,R*64),R*64),:]
            f=left(ax,[f[r]*kk[64*r:64*r+64] for r in range(R)])
            for r in range(R): sb[j,pl.ds(i*R+r,64,stride=32),:]=f[r]
            return c
        lax.fori_loop(0,32//R,half,0)
    def inv(js,q,first):
        b=[]
        for j in js:
            sv=sb[j,rows(q),:]
            for p in range(CP):
                u,v=half_swap(sv[64*p:64*p+32],sv[64*p+32:64*p+64],mask)
                b.append(jnp.concatenate([u,v],0))
        x=lanes(jnp.concatenate(left(ay,b),0),wz)
        acc=None if first else e[rows(q),:]
        for n,j in enumerate(js):
            out=[]
            for p in range(CP):
                k=64*(n*CP+p)
                out+=half_swap(x[k:k+32],x[k+32:k+64],mask)
            term=jnp.concatenate(out,0)*ob[j,rows(q),:]
            acc=-term if acc is None else acc-term
        e[rows(q),:]=acc
    def chunks(f):
        def body(q,c):
            f(q)
            return c
        lax.fori_loop(0,CH,body,0)
    def push(dst_dev,slot,q,rsem,src):
        return pltpu.make_async_remote_copy(src_ref=src.at[rows(q),:],dst_ref=ob.at[slot,rows(q),:],send_sem=osend,recv_sem=rsem.at[q],device_id=dst_dev,device_id_type=MESH)
    def arrive(slot,q,rsem):
        pltpu.make_async_copy(ob.at[slot,rows(q),:],ob.at[slot,rows(q),:],rsem.at[q]).wait()
    pl.semaphore_wait(bar,NDEV-1)
    def start_occ(q):
        push(outer,2,q,brecv,o_ref).start()
        push(across,3,q,crecv,o_ref).start()
        push(inner,1,q,arecv,o_ref).start()
    chunks(start_occ)
    def piece(buf,d):
        return buf.at[pl.ds(pl.multiple_of(lax.rem(d,64)*32+(d//64)*16,16),16),:]
    mine=pl.ds(pl.multiple_of(me*16,16),16)
    def t_send(k,c):
        d=lax.rem(me+k,NDEV)
        pltpu.make_async_remote_copy(src_ref=piece(t_ref,d),dst_ref=tc.at[mine,:],send_sem=tsend,recv_sem=trecv,device_id=peer(d),device_id_type=MESH).start()
        return c
    pltpu.make_async_copy(piece(t_ref,me),tc.at[mine,:],trecv).start()
    chunks(lambda q: fwd(0,q))
    mid(0)
    chunks(lambda q: inv([0],q,True))
    def in_a(q):
        arrive(1,q,arecv)
        fwd(1,q)
    chunks(in_a)
    mid(1)
    chunks(lambda q: inv([1],q,False))
    def in_bcd(q):
        arrive(2,q,brecv)
        push(inner,4,q,drecv,ob.at[2]).start()
        fwd(2,q)
        arrive(3,q,crecv)
        fwd(3,q)
        lax.fori_loop(jnp.maximum(32*q,1),32*q+32,t_send,0)
        arrive(4,q,drecv)
        fwd(4,q)
    chunks(in_bcd)
    def mids(j,c):
        mid(j)
        return c
    lax.fori_loop(2,5,mids,0)
    def e_send(k,c):
        d=lax.rem(k,2)*64+k//2
        src=piece(e,d)
        @pl.when(d==me)
        def _(): pltpu.make_async_copy(src,ec.at[mine,:],erecv).start()
        @pl.when(d!=me)
        def _(): pltpu.make_async_remote_copy(src_ref=src,dst_ref=ec.at[mine,:],send_sem=esend,recv_sem=erecv,device_id=peer(d),device_id_type=MESH).start()
        return c
    def tail(q):
        inv([2,3,4],q,False)
        lax.fori_loop(q*4*CP,(q+1)*4*CP,e_send,0)
    chunks(tail)
    whole=lambda buf,n,sem: pltpu.make_async_copy(buf.at[pl.ds(0,n),:],buf.at[pl.ds(0,n),:],sem).wait()
    whole(tc,2048,trecv); whole(tc,2032,tsend)
    whole(ec,2048,erecv); whole(ec,2032,esend)
    for _ in range(4): whole(e,2048,osend)

VM=pl.BlockSpec(memory_space=pltpu.VMEM)
def k1_call(t,o):
    tabs=[jnp.asarray(a) for a in tables()]
    D=pltpu.SemaphoreType.DMA
    big=lambda *n: pltpu.VMEM(n+(2048,128),F32)
    return pl.pallas_call(k1,out_shape=[jax.ShapeDtypeStruct((2048,128),F32)]*2,in_specs=[VM]*6,out_specs=[VM]*2,
      scratch_shapes=[big(5),big(5),big(),big(),D,D((CH,)),D((CH,)),D((CH,)),D((CH,)),D,D,D,D,D],
      compiler_params=pltpu.CompilerParams(collective_id=0,has_side_effects=True,vmem_limit_bytes=40<<20))(t,o,*tabs)

def home(k):
    o=2*(k%32)
    g=(k//32+k%32+(k%32)//4+(k%32)//16)%2
    return g,o
def ar_kernel(n, x_ref, out_ref, parts, sums, ssem, rsem, gsem, hsem):
    g=lax.axis_index("grp"); o=lax.axis_index("orb")
    me=g*64+o
    bar=pltpu.get_barrier_semaphore()
    def sig(k,c):
        d=lax.rem(me+k,128)
        pl.semaphore_signal(bar,inc=1,device_id=(d//64,lax.rem(d,64)),device_id_type=MESH)
        return c
    lax.fori_loop(1,128,sig,0)
    pl.semaphore_wait(bar,127)
    def tile_of(k):
        hg,ho=home(k)
        return hg,ho,(hg==g)&(ho==o)
    def send(k,c):
        hg,ho,mine=tile_of(k)
        src=x_ref.at[pl.ds(pl.multiple_of(k*8,8),8),:]
        @pl.when(mine)
        def _(): pltpu.make_async_copy(src,parts.at[me],rsem).start()
        @pl.when(jnp.logical_not(mine))
        def _(): pltpu.make_async_remote_copy(src_ref=src,dst_ref=parts.at[me],send_sem=ssem,recv_sem=rsem,device_id=(hg,ho),device_id_type=MESH).start()
        return c
    lax.fori_loop(0,n,send,0)
    def work(k,c):
        hg,ho,mine=tile_of(k)
        @pl.when(mine)
        def _():
            pltpu.make_async_copy(parts,parts,rsem).wait()
            sums[...]=jnp.sum(parts[...],axis=0)
            dst=out_ref.at[pl.ds(pl.multiple_of(k*8,8),8),:]
            pltpu.make_async_copy(sums,dst,hsem).start()
            def bc(j,c2):
                d=lax.rem(me+j,128)
                pltpu.make_async_remote_copy(src_ref=sums,dst_ref=dst,send_sem=gsem,recv_sem=hsem,device_id=(d//64,lax.rem(d,64)),device_id_type=MESH).start()
                return c2
            lax.fori_loop(1,128,bc,0)
        return c
    lax.fori_loop(0,n,work,0)
    pltpu.make_async_copy(out_ref,out_ref,hsem).wait()
    def drain(k,c):
        hg,ho,mine=tile_of(k)
        @pl.when(jnp.logical_not(mine))
        def _():
            pltpu.make_async_copy(sums,sums,ssem).wait()
        @pl.when(mine)
        def _():
            pltpu.make_async_copy(parts.at[pl.ds(0,127)],parts.at[pl.ds(0,127)],gsem).wait()
        return c
    lax.fori_loop(0,n,drain,0)
def all_reduce(x, cid=0):
    n=x.shape[0]//8
    vm=pl.BlockSpec(memory_space=pltpu.VMEM)
    return pl.pallas_call(functools.partial(ar_kernel,n),out_shape=jax.ShapeDtypeStruct(x.shape,F32),
      in_specs=[vm],out_specs=vm,
      scratch_shapes=[pltpu.VMEM((128,8,128),F32),pltpu.VMEM((8,128),F32)]+[pltpu.SemaphoreType.DMA]*4,
      compiler_params=pltpu.CompilerParams(collective_id=cid,has_side_effects=True))(x)

STEP_SIZE = 0.3


def swapped(x, axis):
    return lax.ppermute(x, axis, [(0, 1), (1, 0)])


HI = lax.Precision.HIGHEST


def mm(a, b):
    return jnp.dot(a, b, precision=HI)


def mmt(a, b):
    return lax.dot_general(a, b, (((1,), (1,)), ((), ())), precision=HI)


def on_device(occupied, targets, potential):
    g = lax.axis_index("grp")
    T, E = k1_call(targets.reshape(2048, 128), occupied.reshape(2048, 128))
    T = T.reshape(128, 2048)
    E = E.reshape(128, 2048)
    v = lax.dynamic_slice_in_dim(potential, g * 2048, 2048, 0)
    VT = v[None, :] * T
    grams = jnp.concatenate([mmt(E, E), mmt(T, E), mmt(VT, T)], 0) / CELLS
    grams = all_reduce(grams, 1)
    gee, gte, gvt = grams[:128], grams[128:256], grams[256:]
    factor = jnp.linalg.cholesky(gee)
    half = lax.linalg.triangular_solve(factor, gte.T, left_side=True, lower=True)
    mt = lax.linalg.triangular_solve(factor, half, left_side=True, lower=True, transpose_a=True)
    ray = gvt - mm(half.T, half)
    coeff = jnp.concatenate([mt.T, ray], 1)
    both = jnp.concatenate([E, T], 0)

    def rows_of(which):
        c = lax.dynamic_slice_in_dim(coeff, which * 64, 64, 0)
        old = lax.dynamic_slice_in_dim(T, which * 64, 64, 0)
        return old - STEP_SIZE * (v[None, :] * old - mm(c, both))

    theirs = rows_of(1 - g)
    received = swapped(theirs, "grp")
    mine = rows_of(g)
    return jnp.where(g == 0, jnp.concatenate([mine, received], 1), jnp.concatenate([received, mine], 1))


def solution(mesh):
    placed = (P("orb", None), P(("grp", "orb"), None), P("orb"))
    return jax.shard_map(
        on_device, mesh=mesh, in_specs=placed, out_specs=P("grp", "orb"), check_vma=False
    )
```

profile of v0, /device:TPU:1, one launch (start us, length us, event | category | flops | bytes accessed | tf_op | source)
XLA Modules:
  0.0 150.6 jit_solution(3688113719586068251)
XLA Ops:
  0.0 1.2 copy-done
  1.2 1.2 copy-done.1
  2.5 0.9 copy-done.2
  3.4 0.8 copy-done.3
  4.2 0.8 copy-done.4
  5.7 62.4 %shard_map.73 = (f32[2048,128]{1,0:T(8,128)S(1)}, f32[2048,128]{1,0:T(8,128)S(1)}) custom-call(f32[2048,128]{1,0:T(8,128)S(1)} %bitcast.28, f32[2048,128]{1,0:T(8,128)S(1)} %bitcast.29, bf16[64,192]{1,0:T(8,128)(2,1)S(1)} %copy-done.4, bf16[64,192]{1,0:T(8,128)(2,1)S(1)} %copy-done.5, bf16[256,256]{1,0:T(8,128)(2,1)S(1)} %copy-done.2, f32[96,128]{1,0:T(8,128)S(1)} %copy-done.3), custom_call_target="tpu_custom_call" | custom-call | tf_op jit(solution)/shard_map/pallas_call | solution.py:181
  68.3 1.0 bitcast_multiply_fusion
  69.3 2.3 %mul.54 = f32[128,2048]{1,0:T(8,128)} reshape(f32[2048,128]{1,0:T(8,128)} %bitcast_multiply_fusion) | data formatting | bytes 2097152 | tf_op jit(solution)/shard_map/mul | solution.py:269
  71.8 1.0 fusion.19
  72.8 1.0 fusion.20
  73.8 1.0 fusion.21
  75.5 28.4 %shard_map.74 = f32[384,128]{1,0:T(8,128)} custom-call(f32[384,128]{1,0:T(8,128)} %maximum_multiply_fusion.x_ref), custom_call_target="tpu_custom_call" | custom-call | tf_op jit(solution)/shard_map/pallas_call | solution.py:240
  103.9 0.8 slice.23
  104.9 0.9 fusion.13
  105.7 11.7 %cholesky.16 = f32[128,128]{1,0:T(8,128)S(1)} custom-call(f32[128,128]{1,0:T(8,128)S(1)} %fusion.13), custom_call_target="Cholesky" | custom-call | tf_op jit(solution)/shard_map/jit(cholesky)/cholesky | solution.py:273
  118.8 9.8 %custom-call.8 = f32[1,128,128]{1,2,0:T(8,128)S(1)} custom-call(f32[1,128,128]{2,1,0:T(8,128)S(1)} %fusion.4), custom_call_target="InvertDiagBlocksLowerTriangular" | custom-call | tf_op jit(solution)/shard_map/triangular_solve | solution.py:275
  128.6 1.1 fusion.11
  129.7 1.1 convolution_subtract_fusion.2
  131.2 1.0 constant_dynamic-update-slice_fusion.1
  132.2 1.1 constant_dynamic-update-slice_fusion
  133.3 3.0 %fusion.3 = f32[64,2048]{1,0:T(8,128)S(1)} fusion(f32[256,2048]{1,0:T(8,128)} %constant_dynamic-update-slice_fusion, f32[128,2048]{1,0:T(8,128)S(1)} %reshape.29, s32[]{:T(128)S(6)} %select_n.27, f32[2048]{0:T(1024)S(1)} %dynamic_slice.16, f32[128,128]{1,0:T(8,128)S(1)} %fusion.9, f32[128,128]{1,0:T(8,128)S(1)} %convolution_subtract_fusion.2), kind=kOutput, calls=%fused_computation.5 | convolution fusion | flops 403193856 | bytes 3286016 | tf_op jit(solution)/shard_map/dot_general | solution.py:256
  136.6 3.0 %fusion.1 = f32[64,2048]{1,0:T(8,128)S(1)} fusion(f32[256,2048]{1,0:T(8,128)} %constant_dynamic-update-slice_fusion, f32[128,2048]{1,0:T(8,128)S(1)} %reshape.29, s32[]{:T(128)S(6)} %select_n.24, f32[2048]{0:T(1024)S(1)} %dynamic_slice.16, f32[128,128]{1,0:T(8,128)S(1)} %fusion.9, f32[128,128]{1,0:T(8,128)S(1)} %convolution_subtract_fusion.2), kind=kOutput, calls=%fused_computation.3 | convolution fusion | flops 403193856 | bytes 3286016 | tf_op jit(solution)/shard_map/dot_general | solution.py:256
  139.6 9.8 %collective-permute-done = f32[64,2048]{1,0:T(8,128)S(1)} collective-permute-done((f32[64,2048]{1,0:T(8,128)S(1)}, f32[64,2048]{1,0:T(8,128)S(1)}, u32[]{:S(2)}, u32[]{:S(2)}) %collective-permute-start) | collective-permute-done | bytes 524320 | tf_op jit(solution)/shard_map/ppermute | solution.py:249
  149.5 1.1 maximum_select_fusion
  (22 shorter events, 3.9 us)
Async XLA Ops:
  0.0 1.2 copy-start
  1.2 1.2 copy-start.1
  2.5 0.9 copy-start.2
  3.4 0.8 copy-start.3
  4.2 0.8 copy-start.4
  4.9 0.8 copy-start.5
  5.7 62.6 %copy-start.7 = (f32[4096]{0:T(1024)S(1)}, f32[4096]{0:T(1024)}, u32[]{:S(2)}) copy-start(f32[4096]{0:T(1024)} %param.9) | copy-start | bytes 49156
  71.8 2.0 %copy-start.6 = (f32[128,2048]{1,0:T(8,128)S(1)}, f32[128,2048]{1,0:T(8,128)}, u32[]{:S(2)}) copy-start(f32[128,2048]{1,0:T(8,128)} %mul.54) | copy-start | bytes 3145732
  136.3 13.2 %collective-permute-start = (f32[64,2048]{1,0:T(8,128)S(1)}, f32[64,2048]{1,0:T(8,128)S(1)}, u32[]{:S(2)}, u32[]{:S(2)}) collective-permute-start(f32[64,2048]{1,0:T(8,128)S(1)} %fusion.3), channel_id=1, source_target_pairs={{0,64},{64,0},{1,65},{65,1},{2,66},{66,2},{3,67},{67,3},{4,68},{68... | collective-permute-start | bytes 1572872 | tf_op jit(solution)/shard_map/ppermute | solution.py:249
where the time goes:
time: 151 us
  Pallas kernels  90.8 us (60%)
  other arithmetic  26.6 us (18%)
  local copies, waits for them, and re-layouts  11.4 us (8%)
  matrix products  11.4 us (8%)
  waiting for transfers between devices  9.85 us (7%)
    pallas_call x1, Pallas kernels, k1_call(): pl.pallas_call(k1, out_shape=[jax.ShapeDtypeStruct((2048, 128), F32)] * 2...  62.4 us
    pallas_call x1, Pallas kernels, all_reduce(): pl.pallas_call(functools.partial(ar_kernel, n), out_shape=jax.ShapeDtypeS...  28.4 us
    another operation x3, other arithmetic, on_device(): factor = jnp.linalg.cholesky(gee)  12.4 us
    another operation x2, other arithmetic, on_device(): lax.linalg.triangular_solve(factor, half, left_side=True, lower=True, tra...  10.5 us
    ppermute x1, waiting for transfers between devices, swapped(): return lax.ppermute(x, axis, [(0, 1), (1, 0)])  9.85 us
    dot_general x3, matrix products, mm(): return jnp.dot(a, b, precision=HI)  7.05 us
    unnamed x18, local copies, waits for them, and re-layouts  6.8 us
  transfers between devices with their start and end apart: 1, of which 1 were waited for; matrix products, arithmetic and copies ran while one was open for 2% of the time, Pallas kernels for 0%

commit v1 on v0

v1 whole, which is shorter than its diff:
```python
import functools
import ml_dtypes
import jax
import jax.numpy as jnp
from jax.sharding import PartitionSpec as P
from jax import lax
from jax.experimental import pallas as pl
from jax.experimental.pallas import tpu as pltpu
import numpy as np
BF=jnp.bfloat16; F32=jnp.float32
MESH=pl.DeviceIdType.MESH
CELLS=262144
NDEV=128
CH=4
CP=32//CH
CR=2048//CH

def tables():
    bf=ml_dtypes.bfloat16
    i=np.arange(64)
    ang=2*np.pi*((i[:,None]*i[None,:])%64)/64
    H=(np.cos(ang)+np.sin(ang)).astype(np.float32)
    Hh=H.astype(bf); Hl=(H-Hh.astype(np.float32)).astype(bf)
    perm=2*(i%32)+i//32
    ax=np.concatenate([Hh,Hh,Hl],1)
    ay=ax.reshape(64,3,64)[perm][:,:,perm].reshape(64,192)
    z=np.zeros((64,64),bf)
    bd=lambda m: np.block([[m,z],[z,m]])
    row=np.concatenate([bd(Hh),bd(Hl)],1)
    wz=np.concatenate([row,row],0)
    q=np.minimum(i,64-i).astype(np.float32)*np.float32(2*np.pi/20.0); q2=q*q
    qa=np.broadcast_to((q2+np.float32(0.04))[:,None],(64,128))
    qb=q2.reshape(32,2)
    qr=(qb[:,:,None]+q2[None,None,:]).reshape(32,128)
    return ax,ay,wz,np.concatenate([qa,qr],0).astype(np.float32)

def split(x):
    h=x.astype(BF)
    return h,(x-h.astype(F32)).astype(BF)
def dot(a,b): return jnp.dot(a,b,preferred_element_type=F32)
def half_swap(lo,hi,mask):
    return jnp.where(mask,lo,pltpu.roll(hi,64,1)), jnp.where(mask,pltpu.roll(lo,64,1),hi)
def left(A,planes):
    out=[]
    for k in range(0,len(planes),2):
        h,l=split(jnp.concatenate(planes[k:k+2],1))
        r=dot(A,jnp.concatenate([h,l,h],0))
        out+=[r[:,:128],r[:,128:]]
    return out
def lanes(x,W):
    h,l=split(x)
    r=dot(jnp.concatenate([h,l],1),W)
    return r[:,:128]+r[:,128:]

def peer(d): return (lax.div(d,64),lax.rem(d,64))

def spd_inverse(G):
    n=128
    ri=lax.broadcasted_iota(jnp.int32,(n,n),0); ci=lax.broadcasted_iota(jnp.int32,(n,n),1)
    dg=jnp.where(ri==ci,G,0.0)
    dr=lax.rsqrt(jnp.sum(dg,axis=0,keepdims=True)); dc=lax.rsqrt(jnp.sum(dg,axis=1,keepdims=True))
    sc=dr*dc
    A=G*sc
    lane=lax.broadcasted_iota(jnp.int32,(1,n),1); sub=lax.broadcasted_iota(jnp.int32,(n,1),0)
    for k in range(n):
        r=A[k:k+1,:]; c=A[:,k:k+1]; d=A[k:k+1,k:k+1]
        v=(r+(lane==k).astype(F32))*(1.0/d)
        u=c-(sub==k).astype(F32)
        A=A-u*v
    return A*sc


def home(k):
    o=2*lax.rem(k,32)
    g=lax.rem(lax.div(k,32)+lax.rem(k,32)+lax.div(lax.rem(k,32),4)+lax.div(lax.rem(k,32),16),2)
    return g*64+o

def mega(t_hbm,o_hbm,p_hbm,ax_hbm,ay_hbm,wz_hbm,q_hbm,out,tc,ec,t_ref,vp,ax_ref,ay_ref,wz_ref,q_ref,xh,xl,part,gs,parts,sums,ub,ob,sb,kt,e,osend,arecv,brecv,crecv,drecv,tsend,trecv,esend,erecv,loc,tabs,rsend,rrecv,gsend,grecv,usend,urecv):
    g=lax.axis_index("grp"); o=lax.axis_index("orb"); me=g*64+o
    s=2*lax.rem(o,2)-1
    w=lambda v: lax.rem(v+128,64)
    inner=(g,w(o-s)); outer=(g,w(o+s)); across=(g,w(o-2*s))
    copies=[pltpu.make_async_copy(a,b,tabs.at[i]) for i,(a,b) in enumerate(((q_hbm,q_ref),(o_hbm,ob.at[0]),(t_hbm,t_ref),(ax_hbm,ax_ref),(ay_hbm,ay_ref),(wz_hbm,wz_ref),(p_hbm,vp)))]
    for c in copies: c.start()
    bar=pltpu.get_barrier_semaphore()
    def sig(k,c):
        pl.semaphore_signal(bar,inc=1,device_id=peer(lax.rem(me+k,NDEV)),device_id_type=MESH)
        return c
    lax.fori_loop(1,NDEV,sig,0)
    mask=lax.broadcasted_iota(jnp.int32,(32,128),1)<64
    copies[0].wait()
    qa=q_ref[0:64,:]
    def ktab(r,c):
        kt[pl.ds(pl.multiple_of(r*64,64),64),:]=(4*np.pi/CELLS)/(qa+q_ref[pl.ds(64+r,1),:])
        return c
    lax.fori_loop(0,32,ktab,0,unroll=8)
    for c in copies[1:]: c.wait()
    ax=ax_ref[...];ay=ay_ref[...];wz=wz_ref[...]
    o_ref=ob.at[0]
    def rows(q): return pl.ds(pl.multiple_of(q*CR,CR),CR)
    def fwd(j,q):
        pr=t_ref[rows(q),:]*ob[j,rows(q),:]
        b=[]
        for p in range(CP):
            b+=half_swap(pr[64*p:64*p+32],pr[64*p+32:64*p+64],mask)
        x=lanes(jnp.concatenate(b,0),wz)
        f=left(ay,[x[64*p:64*p+64] for p in range(CP)])
        out=[]
        for p in range(CP): out+=half_swap(f[p][:32],f[p][32:],mask)
        sb[j,rows(q),:]=jnp.concatenate(out,0)
    R=16
    def mid(j):
        def half(i,c):
            f=left(ax,[sb[j,pl.ds(i*R+r,64,stride=32),:] for r in range(R)])
            kk=kt[pl.ds(pl.multiple_of(i*R*64,R*64),R*64),:]
            f=left(ax,[f[r]*kk[64*r:64*r+64] for r in range(R)])
            for r in range(R): sb[j,pl.ds(i*R+r,64,stride=32),:]=f[r]
            return c
        lax.fori_loop(0,32//R,half,0)
    def inv(js,q,first):
        b=[]
        for j in js:
            sv=sb[j,rows(q),:]
            for p in range(CP):
                u,v=half_swap(sv[64*p:64*p+32],sv[64*p+32:64*p+64],mask)
                b.append(jnp.concatenate([u,v],0))
        x=lanes(jnp.concatenate(left(ay,b),0),wz)
        acc=None if first else e[rows(q),:]
        for n,j in enumerate(js):
            out=[]
            for p in range(CP):
                k=64*(n*CP+p)
                out+=half_swap(x[k:k+32],x[k+32:k+64],mask)
            term=jnp.concatenate(out,0)*ob[j,rows(q),:]
            acc=-term if acc is None else acc-term
        e[rows(q),:]=acc
    def chunks(f):
        def body(q,c):
            f(q)
            return c
        lax.fori_loop(0,CH,body,0)
    def push(dst_dev,slot,q,rsem,src):
        return pltpu.make_async_remote_copy(src_ref=src.at[rows(q),:],dst_ref=ob.at[slot,rows(q),:],send_sem=osend,recv_sem=rsem.at[q],device_id=dst_dev,device_id_type=MESH)
    def arrive(slot,q,rsem):
        pltpu.make_async_copy(ob.at[slot,rows(q),:],ob.at[slot,rows(q),:],rsem.at[q]).wait()
    pl.semaphore_wait(bar,NDEV-1)
    def start_occ(q):
        push(outer,2,q,brecv,o_ref).start()
        push(across,3,q,crecv,o_ref).start()
        push(inner,1,q,arecv,o_ref).start()
    chunks(start_occ)
    def piece(buf,d):
        return buf.at[pl.ds(pl.multiple_of(lax.rem(d,64)*32+lax.div(d,64)*16,16),16),:]
    mine=pl.ds(pl.multiple_of(me*16,16),16)
    def t_send(k,c):
        d=lax.rem(me+k,NDEV)
        pltpu.make_async_remote_copy(src_ref=piece(t_ref,d),dst_ref=tc.at[mine,:],send_sem=tsend,recv_sem=trecv,device_id=peer(d),device_id_type=MESH).start()
        return c
    pltpu.make_async_copy(piece(t_ref,me),tc.at[mine,:],trecv).start()
    chunks(lambda q: fwd(0,q))
    mid(0)
    chunks(lambda q: inv([0],q,True))
    def in_a(q):
        arrive(1,q,arecv)
        fwd(1,q)
    chunks(in_a)
    mid(1)
    chunks(lambda q: inv([1],q,False))
    def in_bcd(q):
        arrive(2,q,brecv)
        push(inner,4,q,drecv,ob.at[2]).start()
        fwd(2,q)
        arrive(3,q,crecv)
        fwd(3,q)
        lax.fori_loop(jnp.maximum(32*q,1),32*q+32,t_send,0)
        arrive(4,q,drecv)
        fwd(4,q)
    chunks(in_bcd)
    def mids(j,c):
        mid(j)
        return c
    lax.fori_loop(2,5,mids,0)
    def e_send(k,c):
        d=lax.rem(k,2)*64+lax.div(k,2)
        src=piece(e,d)
        @pl.when(d==me)
        def _(): pltpu.make_async_copy(src,ec.at[mine,:],erecv).start()
        @pl.when(d!=me)
        def _(): pltpu.make_async_remote_copy(src_ref=src,dst_ref=ec.at[mine,:],send_sem=esend,recv_sem=erecv,device_id=peer(d),device_id_type=MESH).start()
        return c
    def tail(q):
        inv([2,3,4],q,False)
        lax.fori_loop(q*4*CP,(q+1)*4*CP,e_send,0)
    chunks(tail)
    whole=lambda buf,n,sem: pltpu.make_async_copy(buf.at[pl.ds(0,n),:],buf.at[pl.ds(0,n),:],sem).wait()
    def spread(lo,hi):
        def send(n,c):
            src=part.at[pl.ds(pl.multiple_of(n*8,8),8),:]
            h=home(n)
            @pl.when(h==me)
            def _(): pltpu.make_async_copy(src,parts.at[me],rrecv).start()
            @pl.when(h!=me)
            def _(): pltpu.make_async_remote_copy(src_ref=src,dst_ref=parts.at[me],send_sem=rsend,recv_sem=rrecv,device_id=peer(h),device_id_type=MESH).start()
            return c
        lax.fori_loop(lo,hi,send,0)
    def nt(a,b): return lax.dot_general(a,b,(((1,),(1,)),((),())),preferred_element_type=F32)
    def rowset(buf,s): return buf[pl.ds(s,128,stride=16),:]
    def vrow(s): return vp[pl.ds(g*16+s,1),:]
    whole(tc,2048,trecv)
    for s in range(16):
        h,l=split(rowset(tc,s))
        xh[128:256,128*s:128*s+128]=h; xl[128:256,128*s:128*s+128]=l
        h,l=split(rowset(tc,s)*vrow(s))
        xh[0:128,128*s:128*s+128]=h; xl[0:128,128*s:128*s+128]=l
    part[256:384,:]=(nt(xh[0:128,:],xh[128:256,:])+nt(xh[0:128,:],xl[128:256,:])+nt(xl[0:128,:],xh[128:256,:]))*(1.0/CELLS)
    spread(32,48)
    whole(ec,2048,erecv)
    for s in range(16):
        h,l=split(rowset(ec,s))
        xh[0:128,128*s:128*s+128]=h; xl[0:128,128*s:128*s+128]=l
    part[0:256,:]=(nt(xh[...],xh[0:128,:])+nt(xh[...],xl[0:128,:])+nt(xl[...],xh[0:128,:]))*(1.0/CELLS)
    spread(0,32)
    def gather(n,c):
        @pl.when(home(n)==me)
        def _():
            pltpu.make_async_copy(parts,parts,rrecv).wait()
            sums[...]=jnp.sum(parts[...],axis=0)
            dst=gs.at[pl.ds(pl.multiple_of(n*8,8),8),:]
            pltpu.make_async_copy(sums,dst,grecv).start()
            def bc(j,c2):
                pltpu.make_async_remote_copy(src_ref=sums,dst_ref=dst,send_sem=gsend,recv_sem=grecv,device_id=peer(lax.rem(me+j,NDEV)),device_id_type=MESH).start()
                return c2
            lax.fori_loop(1,NDEV,bc,0)
        return c
    lax.fori_loop(0,48,gather,0)
    pltpu.make_async_copy(gs,gs,grecv).wait()
    HI=lax.Precision.HIGHEST
    gte=gs[128:256,:]
    m=jnp.dot(gte,spd_inverse(gs[0:128,:]),precision=HI,preferred_element_type=F32)
    ray=gs[256:384,:]-lax.dot_general(m,gte,(((1,),(1,)),((),())),precision=HI,preferred_element_type=F32)
    ch,cl=split(jnp.concatenate([m,ray],1))
    sb[0,0:128,:]=m; sb[0,128:256,:]=ray
    def coeff(which):
        b=which*64
        h0,l0=split(sb[0,pl.ds(pl.multiple_of(b,64),64),:]); h1,l1=split(sb[0,pl.ds(pl.multiple_of(128+b,64),64),:])
        return jnp.concatenate([h0,h1],1),jnp.concatenate([l0,l1],1)
    def rows_of(which,s,n):
        h,l=coeff(which)
        c=slice(128*s,128*(s+n))
        r=dot(h,xh[:,c])+dot(h,xl[:,c])+dot(l,xh[:,c])
        old=jnp.concatenate([tc[pl.ds(which*1024+s+i,64,stride=16),:] for i in range(n)],1)
        v=jnp.concatenate([vrow(s+i) for i in range(n)],1)
        return old-0.3*(v*old-r)
    other=1-g
    cols=lambda s,n: pl.ds(pl.multiple_of(g*2048+128*s,128),128*n)
    N=4
    def swap_copy(s): return pltpu.make_async_remote_copy(src_ref=ub.at[:,pl.ds(128*s,128*N)],dst_ref=out.at[:,cols(s,N)],send_sem=usend.at[s//N],recv_sem=urecv.at[s//N],device_id=(other,o),device_id_type=MESH)
    for s in range(0,16,N):
        ub[:,128*s:128*(s+N)]=rows_of(other,s,N)
        swap_copy(s).start()
    for s in range(0,16,N):
        out[:,cols(s,N)]=rows_of(g,s,N)
    for s in range(0,16,N): swap_copy(s).wait()
    def drain(n,c):
        @pl.when(home(n)!=me)
        def _(): pltpu.make_async_copy(sums,sums,rsend).wait()
        @pl.when(home(n)==me)
        def _(): pltpu.make_async_copy(parts.at[pl.ds(0,127)],parts.at[pl.ds(0,127)],gsend).wait()
        return c
    lax.fori_loop(0,48,drain,0)
    whole(tc,2032,tsend); whole(ec,2032,esend)
    for _ in range(4): whole(e,2048,osend)

VM=pl.BlockSpec(memory_space=pltpu.VMEM)
ANY=pl.BlockSpec(memory_space=pl.ANY)
def mega_call(t,o,p):
    tabs=[jnp.asarray(a) for a in tables()]
    D=pltpu.SemaphoreType.DMA
    big=lambda *n: pltpu.VMEM(n+(2048,128),F32)
    return pl.pallas_call(mega,out_shape=jax.ShapeDtypeStruct((64,4096),F32),in_specs=[ANY]*7,out_specs=VM,
      scratch_shapes=[big(),big(),big(),pltpu.VMEM((32,128),F32),pltpu.VMEM((64,192),BF),pltpu.VMEM((64,192),BF),pltpu.VMEM((256,256),BF),pltpu.VMEM((96,128),F32),
        pltpu.VMEM((256,2048),BF),pltpu.VMEM((256,2048),BF),pltpu.VMEM((384,128),F32),pltpu.VMEM((384,128),F32),pltpu.VMEM((128,8,128),F32),pltpu.VMEM((8,128),F32),pltpu.VMEM((64,2048),F32),
        big(5),big(5),big(),big(),D,D((CH,)),D((CH,)),D((CH,)),D((CH,)),D,D,D,D,D,D((7,)),D,D,D,D,D((4,)),D((4,))],
      compiler_params=pltpu.CompilerParams(collective_id=0,has_side_effects=True,vmem_limit_bytes=58<<20))(t,o,p,*tabs)

def on_device(occupied, targets, potential):
    return mega_call(targets.reshape(2048, 128), occupied.reshape(2048, 128), potential.reshape(32, 128))


def solution(mesh):
    placed = (P("orb", None), P(("grp", "orb"), None), P("orb"))
    return jax.shard_map(
        on_device, mesh=mesh, in_specs=placed, out_specs=P("grp", "orb"), check_vma=False
    )
```

time: 151 us -> 110 us (0.73)
  other arithmetic: 26.6 us -> 0 us
  Pallas kernels: 90.8 us -> 108 us
  matrix products: 11.4 us -> 0 us
  waiting for transfers between devices: 9.85 us -> 0 us
  local copies, waits for them, and re-layouts: 11.4 us -> 2.27 us
    another operation x5 -> x0, other arithmetic: 22.9 us -> none  [the longest x3 12.4 us: on_device(): factor = jnp.linalg.cholesky(gee)]
    pallas_call x2 -> x1, Pallas kernels: 90.8 us -> 108 us  [mega_call(): pl.pallas_call(mega, out_shape=jax.ShapeDtypeStruct((64, 4096), F32), in_...]
    dot_general x6 -> x0, matrix products: 10 us -> none  [the longest x3 7.05 us: mm(): return jnp.dot(a, b, precision=HI)]
    ppermute x1 -> x0, waiting for transfers between devices: 9.85 us -> none  [swapped(): return lax.ppermute(x, axis, [(0, 1), (1, 0)])]
    unnamed x18 -> x1, local copies, waits for them, and re-layouts: 6.8 us -> 2.27 us
    mul x2 -> x0, local copies, waits for them, and re-layouts: 2.36 us -> none  [on_device(): VT = v[None, :] * T]
    div x2 -> x0, other arithmetic: 1.55 us -> none  [the longest x1 0.86 us: on_device(): factor = jnp.linalg.cholesky(gee)]
  transfers between devices with their start and end apart: 1 -> 0, of which waited for: 1 -> 0; matrix products, arithmetic and copies ran while one was open for 2% -> 0% of each run, Pallas kernels for 0% -> 0%
where the time goes in v1:
time: 110 us
  Pallas kernels  108 us (98%)
  local copies, waits for them, and re-layouts  2.27 us (2%)
    pallas_call x1, Pallas kernels, mega_call(): pl.pallas_call(mega, out_shape=jax.ShapeDtypeStruct((64, 4096), F32), in_...  108 us
    unnamed x1, local copies, waits for them, and re-layouts  2.27 us

profile of v1, /device:TPU:1, one launch (start us, length us, event | category | flops | bytes accessed | tf_op | source)
XLA Modules:
  0.0 110.4 jit_solution(13790259410635601930)
XLA Ops:
  0.0 108.1 %shard_map.73 = f32[64,4096]{1,0:T(8,128)} custom-call(f32[2048,128]{1,0:T(8,128)} %bitcast.3, f32[2048,128]{1,0:T(8,128)} %bitcast.4, f32[32,128]{1,0:T(8,128)} %bitcast.5, bf16[64,192]{1,0:T(8,128)(2,1)} %constant.8.clone.ax_hbm, bf16[64,192]{1,0:T(8,128)(2,1)} %constant.9.clone.ay_hbm, bf16[256,256]{1,0:T(8,128)(2,1)} %constant.10.clone.wz_hbm, ...), custom_call_target="tpu_custom_call" | custom-call | tf_op jit(solution)/shard_map/pallas_call | solution.py:280
  108.1 2.3 %copy.9 = f32[64,4096]{1,0:T(8,128)} copy(f32[64,4096]{1,0:T(8,128)} %shard_map.73) | data formatting | bytes 2097152

commit v2 on v1

--- a/solution.py
+++ b/solution.py
@@ -54,20 +54,57 @@
 
 def peer(d): return (lax.div(d,64),lax.rem(d,64))
 
+NB=8
+def recip(x):
+    y=pl.reciprocal(x,approx=True)
+    y=y*(2.0-x*y)
+    return y*(2.0-x*y)
+def block_cols(Bp,k,sub):
+    a={}
+    for i in range(NB):
+        for j in range(i,NB):
+            a[i,j]=jnp.broadcast_to(Bp[i:i+1,k+j:k+j+1],(NB,128))
+    g=lambda i,j: a[min(i,j),max(i,j)]
+    for q in range(NB):
+        rd=recip(a[q,q])
+        c=[g(i,q) for i in range(NB)]
+        t=[c[i]*rd for i in range(NB)]
+        for i in range(NB):
+            for j in range(i,NB):
+                if i!=q and j!=q: a[i,j]=a[i,j]-c[i]*t[j]
+        for i in range(NB):
+            if i!=q: a[min(i,q),max(i,q)]=t[i]
+        a[q,q]=-rd
+    cols=[]
+    for j in range(NB):
+        v=g(0,j)
+        for i in range(1,NB): v=jnp.where(sub==i,g(i,j),v)
+        cols.append(-v)
+    return cols
+def tree(xs):
+    while len(xs)>1: xs=[xs[i]+xs[i+1] if i+1<len(xs) else xs[i] for i in range(0,len(xs),2)]
+    return xs[0]
+
 def spd_inverse(G):
     n=128
     ri=lax.broadcasted_iota(jnp.int32,(n,n),0); ci=lax.broadcasted_iota(jnp.int32,(n,n),1)
     dg=jnp.where(ri==ci,G,0.0)
-    dr=lax.rsqrt(jnp.sum(dg,axis=0,keepdims=True)); dc=lax.rsqrt(jnp.sum(dg,axis=1,keepdims=True))
-    sc=dr*dc
+    sc=lax.rsqrt(jnp.sum(dg,axis=0,keepdims=True))*lax.rsqrt(jnp.sum(dg,axis=1,keepdims=True))
     A=G*sc
-    lane=lax.broadcasted_iota(jnp.int32,(1,n),1); sub=lax.broadcasted_iota(jnp.int32,(n,1),0)
-    for k in range(n):
-        r=A[k:k+1,:]; c=A[:,k:k+1]; d=A[k:k+1,k:k+1]
-        v=(r+(lane==k).astype(F32))*(1.0/d)
-        u=c-(sub==k).astype(F32)
-        A=A-u*v
-    return A*sc
+    lane=lax.broadcasted_iota(jnp.int32,(8,n),1); sub=lax.broadcasted_iota(jnp.int32,(8,n),0)
+    rows=[A[8*i:8*i+8,:] for i in range(16)]
+    nxt=rows[0]
+    for p in range(16):
+        k=8*p
+        eye=(lane==sub+k).astype(F32)
+        cols=block_cols(nxt,k,sub)
+        R=nxt+eye
+        W=tree([cols[j]*R[j:j+1,:] for j in range(NB)])
+        wj=[W[j:j+1,:] for j in range(NB)]
+        upd=lambda a: a-tree([a[:,k+j:k+j+1]*wj[j] for j in range(NB)])
+        if p<15: nxt=upd(rows[p+1])
+        rows=[W-eye if i==p else nxt if i==p+1 else upd(rows[i]) for i in range(16)]
+    return jnp.concatenate(rows,0)*sc
 
 
 def home(k):
@@ -143,21 +180,38 @@
         return pltpu.make_async_remote_copy(src_ref=src.at[rows(q),:],dst_ref=ob.at[slot,rows(q),:],send_sem=osend,recv_sem=rsem.at[q],device_id=dst_dev,device_id_type=MESH)
     def arrive(slot,q,rsem):
         pltpu.make_async_copy(ob.at[slot,rows(q),:],ob.at[slot,rows(q),:],rsem.at[q]).wait()
+    chunks(lambda q: fwd(0,q))
     pl.semaphore_wait(bar,NDEV-1)
-    def start_occ(q):
-        push(outer,2,q,brecv,o_ref).start()
-        push(across,3,q,crecv,o_ref).start()
-        push(inner,1,q,arecv,o_ref).start()
-    chunks(start_occ)
+    def alone(v):
+        c=lax.rem(lax.div(v,2),16)
+        return ((c==3)|(c==12)).astype(jnp.int32)
+    single=alone(o)
+    def order(i,a=single):
+        f=3*g*(1-a)
+        return i+jnp.where(i==0,f,jnp.where(i==3,-f,0))
+    f3=order(0)
+    on_out,on_across=alone(w(o+s)),alone(w(o-2*s))
+    twin=(1-g,o)
+    def start_a(q): push(inner,1,q,arecv,o_ref).start()
+    def loop(lo,hi,f):
+        def body(i,c):
+            f(i)
+            return c
+        lax.fori_loop(lo,hi,body,0)
+    def start_bc(i):
+        @pl.when(i<3+on_out)
+        def _(): push(outer,2,order(i,on_out),brecv,o_ref).start()
+        @pl.when(i<3+on_across)
+        def _(): push(across,3,order(i,on_across),crecv,o_ref).start()
+    loop(0,4,start_bc)
+    chunks(start_a)
     def piece(buf,d):
         return buf.at[pl.ds(pl.multiple_of(lax.rem(d,64)*32+lax.div(d,64)*16,16),16),:]
     mine=pl.ds(pl.multiple_of(me*16,16),16)
-    def t_send(k,c):
-        d=lax.rem(me+k,NDEV)
+    def t_send(k):
+        d=lax.rem(me+45*k,NDEV)
         pltpu.make_async_remote_copy(src_ref=piece(t_ref,d),dst_ref=tc.at[mine,:],send_sem=tsend,recv_sem=trecv,device_id=peer(d),device_id_type=MESH).start()
-        return c
     pltpu.make_async_copy(piece(t_ref,me),tc.at[mine,:],trecv).start()
-    chunks(lambda q: fwd(0,q))
     mid(0)
     chunks(lambda q: inv([0],q,True))
     def in_a(q):
@@ -165,21 +219,32 @@
         fwd(1,q)
     chunks(in_a)
     mid(1)
+    arrive(2,f3,brecv)
+    @pl.when(single==0)
+    def _(): push(twin,2,f3,brecv,ob.at[2]).start()
+    push(inner,4,f3,drecv,ob.at[2]).start()
+    arrive(3,f3,crecv)
+    @pl.when(single==0)
+    def _(): push(twin,3,f3,crecv,ob.at[3]).start()
     chunks(lambda q: inv([1],q,False))
-    def in_bcd(q):
-        arrive(2,q,brecv)
-        push(inner,4,q,drecv,ob.at[2]).start()
+    def in_bcd(i):
+        q=order(i)
+        @pl.when(i>0)
+        def _():
+            arrive(2,q,brecv)
+            push(inner,4,q,drecv,ob.at[2]).start()
         fwd(2,q)
-        arrive(3,q,crecv)
+        @pl.when(i>0)
+        def _(): arrive(3,q,crecv)
         fwd(3,q)
-        lax.fori_loop(jnp.maximum(32*q,1),32*q+32,t_send,0)
         arrive(4,q,drecv)
         fwd(4,q)
-    chunks(in_bcd)
-    def mids(j,c):
-        mid(j)
-        return c
-    lax.fori_loop(2,5,mids,0)
+    loop(0,3,in_bcd)
+    loop(3,4,in_bcd)
+    loop(1,NDEV,t_send)
+    mid(2)
+    mid(3)
+    mid(4)
     def e_send(k,c):
         d=lax.rem(k,2)*64+lax.div(k,2)
         src=piece(e,d)
@@ -228,9 +293,15 @@
             dst=gs.at[pl.ds(pl.multiple_of(n*8,8),8),:]
             pltpu.make_async_copy(sums,dst,grecv).start()
             def bc(j,c2):
-                pltpu.make_async_remote_copy(src_ref=sums,dst_ref=dst,send_sem=gsend,recv_sem=grecv,device_id=peer(lax.rem(me+j,NDEV)),device_id_type=MESH).start()
+                step=lambda v: jnp.where(v<2,2+v,3-v)
+                dz,dy,dx=step(lax.div(j,32)),step(lax.rem(lax.div(j,8),4)),step(lax.rem(lax.div(j,2),4))
+                y=lax.rem(2*lax.div(o,32)+g+dy,4)
+                z=lax.rem(lax.div(o,8)+dz,4)
+                x=lax.rem(lax.div(o,2)+dx,4)
+                c=lax.rem(o+1+j,2)
+                pltpu.make_async_remote_copy(src_ref=sums,dst_ref=dst,send_sem=gsend,recv_sem=grecv,device_id=(lax.rem(y,2),lax.div(y,2)*32+z*8+x*2+c),device_id_type=MESH).start()
                 return c2
-            lax.fori_loop(1,NDEV,bc,0)
+            lax.fori_loop(0,NDEV-1,bc,0)
         return c
     lax.fori_loop(0,48,gather,0)
     pltpu.make_async_copy(gs,gs,grecv).wait()
@@ -260,7 +331,6 @@
         swap_copy(s).start()
     for s in range(0,16,N):
         out[:,cols(s,N)]=rows_of(g,s,N)
-    for s in range(0,16,N): swap_copy(s).wait()
     def drain(n,c):
         @pl.when(home(n)!=me)
         def _(): pltpu.make_async_copy(sums,sums,rsend).wait()
@@ -269,7 +339,11 @@
         return c
     lax.fori_loop(0,48,drain,0)
     whole(tc,2032,tsend); whole(ec,2032,esend)
-    for _ in range(4): whole(e,2048,osend)
+    def drain_occ(i,c):
+        pltpu.make_async_copy(ob.at[0,rows(0),:],ob.at[0,rows(0),:],osend).wait()
+        return c
+    lax.fori_loop(0,16+on_out+on_across-2*single,drain_occ,0)
+    for s in range(0,16,N): swap_copy(s).wait()
 
 VM=pl.BlockSpec(memory_space=pltpu.VMEM)
 ANY=pl.BlockSpec(memory_space=pl.ANY)

time: 110 us -> 108 us (0.982)
  Pallas kernels: 108 us -> 106 us
    pallas_call x1, Pallas kernels: 108 us -> 106 us  [mega_call(): pl.pallas_call(mega, out_shape=jax.ShapeDtypeStruct((64, 4096), F32), in_...]
where the time goes in v2:
time: 108 us
  Pallas kernels  106 us (98%)
  local copies, waits for them, and re-layouts  2.27 us (2%)
    pallas_call x1, Pallas kernels, mega_call(): pl.pallas_call(mega, out_shape=jax.ShapeDtypeStruct((64, 4096), F32), in_...  106 us
    unnamed x1, local copies, waits for them, and re-layouts  2.27 us

profile of v2, /device:TPU:1, one launch (start us, length us, event | category | flops | bytes accessed | tf_op | source)
XLA Modules:
  0.0 108.2 jit_solution(9610582893293898948)
XLA Ops:
  0.0 106.0 %shard_map.73 = f32[64,4096]{1,0:T(8,128)} custom-call(f32[2048,128]{1,0:T(8,128)} %bitcast.3, f32[2048,128]{1,0:T(8,128)} %bitcast.4, f32[32,128]{1,0:T(8,128)} %bitcast.5, bf16[64,192]{1,0:T(8,128)(2,1)} %constant.8.clone.ax_hbm, bf16[64,192]{1,0:T(8,128)(2,1)} %constant.9.clone.ay_hbm, bf16[256,256]{1,0:T(8,128)(2,1)} %constant.10.clone.wz_hbm, ...), custom_call_target="tpu_custom_call" | custom-call | tf_op jit(solution)/shard_map/pallas_call | solution.py:354
  106.0 2.3 %copy.9 = f32[64,4096]{1,0:T(8,128)} copy(f32[64,4096]{1,0:T(8,128)} %shard_map.73) | data formatting | bytes 2097152

commit v3 on v2

--- a/solution.py
+++ b/solution.py
@@ -306,31 +306,33 @@
     lax.fori_loop(0,48,gather,0)
     pltpu.make_async_copy(gs,gs,grecv).wait()
     HI=lax.Precision.HIGHEST
-    gte=gs[128:256,:]
-    m=jnp.dot(gte,spd_inverse(gs[0:128,:]),precision=HI,preferred_element_type=F32)
-    ray=gs[256:384,:]-lax.dot_general(m,gte,(((1,),(1,)),((),())),precision=HI,preferred_element_type=F32)
-    ch,cl=split(jnp.concatenate([m,ray],1))
-    sb[0,0:128,:]=m; sb[0,128:256,:]=ray
+    def solve_small():
+        gte=gs[128:256,:]
+        m=jnp.dot(gte,spd_inverse(gs[0:128,:]),precision=HI,preferred_element_type=F32)
+        sb[0,0:128,:]=m
+        sb[0,128:256,:]=gs[256:384,:]-lax.dot_general(m,gte,(((1,),(1,)),((),())),precision=HI,preferred_element_type=F32)
+    loop(0,1+lax.div(o,64),lambda i: solve_small())
     def coeff(which):
         b=which*64
         h0,l0=split(sb[0,pl.ds(pl.multiple_of(b,64),64),:]); h1,l1=split(sb[0,pl.ds(pl.multiple_of(128+b,64),64),:])
         return jnp.concatenate([h0,h1],1),jnp.concatenate([l0,l1],1)
-    def rows_of(which,s,n):
+    N=4
+    def rows_of(which,i):
         h,l=coeff(which)
-        c=slice(128*s,128*(s+n))
+        c=pl.ds(pl.multiple_of(i*128*N,128*N),128*N)
         r=dot(h,xh[:,c])+dot(h,xl[:,c])+dot(l,xh[:,c])
-        old=jnp.concatenate([tc[pl.ds(which*1024+s+i,64,stride=16),:] for i in range(n)],1)
-        v=jnp.concatenate([vrow(s+i) for i in range(n)],1)
+        old=jnp.concatenate([tc[pl.ds(which*1024+i*N+n,64,stride=16),:] for n in range(N)],1)
+        v=jnp.concatenate([vrow(i*N+n) for n in range(N)],1)
         return old-0.3*(v*old-r)
     other=1-g
-    cols=lambda s,n: pl.ds(pl.multiple_of(g*2048+128*s,128),128*n)
-    N=4
-    def swap_copy(s): return pltpu.make_async_remote_copy(src_ref=ub.at[:,pl.ds(128*s,128*N)],dst_ref=out.at[:,cols(s,N)],send_sem=usend.at[s//N],recv_sem=urecv.at[s//N],device_id=(other,o),device_id_type=MESH)
-    for s in range(0,16,N):
-        ub[:,128*s:128*(s+N)]=rows_of(other,s,N)
-        swap_copy(s).start()
-    for s in range(0,16,N):
-        out[:,cols(s,N)]=rows_of(g,s,N)
+    part_of=lambda base,i: pl.ds(pl.multiple_of(base+i*128*N,128*N),128*N)
+    def swap_copy(i): return pltpu.make_async_remote_copy(src_ref=ub.at[:,part_of(0,i)],dst_ref=out.at[:,part_of(g*2048,i)],send_sem=usend.at[i],recv_sem=urecv.at[i],device_id=(other,o),device_id_type=MESH)
+    def theirs(i):
+        ub[:,part_of(0,i)]=rows_of(other,i)
+        swap_copy(i).start()
+    loop(0,16//N,theirs)
+    def ours(i): out[:,part_of(g*2048,i)]=rows_of(g,i)
+    loop(0,16//N,ours)
     def drain(n,c):
         @pl.when(home(n)!=me)
         def _(): pltpu.make_async_copy(sums,sums,rsend).wait()
@@ -343,7 +345,7 @@
         pltpu.make_async_copy(ob.at[0,rows(0),:],ob.at[0,rows(0),:],osend).wait()
         return c
     lax.fori_loop(0,16+on_out+on_across-2*single,drain_occ,0)
-    for s in range(0,16,N): swap_copy(s).wait()
+    for i in range(16//N): swap_copy(i).wait()
 
 VM=pl.BlockSpec(memory_space=pltpu.VMEM)
 ANY=pl.BlockSpec(memory_space=pl.ANY)

time: 108 us -> 104 us (0.963)
  Pallas kernels: 106 us -> 102 us
    pallas_call x1, Pallas kernels: 106 us -> 102 us  [mega_call(): pl.pallas_call(mega, out_shape=jax.ShapeDtypeStruct((64, 4096), F32), in_...]
where the time goes in v3:
time: 104 us
  Pallas kernels  102 us (98%)
  local copies, waits for them, and re-layouts  2.27 us (2%)
    pallas_call x1, Pallas kernels, mega_call(): pl.pallas_call(mega, out_shape=jax.ShapeDtypeStruct((64, 4096), F32), in_...  102 us
    unnamed x1, local copies, waits for them, and re-layouts  2.27 us

profile of v3, /device:TPU:1, one launch (start us, length us, event | category | flops | bytes accessed | tf_op | source)
XLA Modules:
  0.0 104.1 jit_solution(3503176564505618724)
XLA Ops:
  0.0 101.8 %shard_map.73 = f32[64,4096]{1,0:T(8,128)} custom-call(f32[2048,128]{1,0:T(8,128)} %bitcast.3, f32[2048,128]{1,0:T(8,128)} %bitcast.4, f32[32,128]{1,0:T(8,128)} %bitcast.5, bf16[64,192]{1,0:T(8,128)(2,1)} %constant.8.clone.ax_hbm, bf16[64,192]{1,0:T(8,128)(2,1)} %constant.9.clone.ay_hbm, bf16[256,256]{1,0:T(8,128)(2,1)} %constant.10.clone.wz_hbm, ...), custom_call_target="tpu_custom_call" | custom-call | tf_op jit(solution)/shard_map/pallas_call | solution.py:356
  101.8 2.3 %copy.9 = f32[64,4096]{1,0:T(8,128)} copy(f32[64,4096]{1,0:T(8,128)} %shard_map.73) | data formatting | bytes 2097152

commit v4 on v3

--- a/solution.py
+++ b/solution.py
@@ -112,7 +112,7 @@
     g=lax.rem(lax.div(k,32)+lax.rem(k,32)+lax.div(lax.rem(k,32),4)+lax.div(lax.rem(k,32),16),2)
     return g*64+o
 
-def mega(t_hbm,o_hbm,p_hbm,ax_hbm,ay_hbm,wz_hbm,q_hbm,out,tc,ec,t_ref,vp,ax_ref,ay_ref,wz_ref,q_ref,xh,xl,part,gs,parts,sums,ub,ob,sb,kt,e,osend,arecv,brecv,crecv,drecv,tsend,trecv,esend,erecv,loc,tabs,rsend,rrecv,gsend,grecv,usend,urecv):
+def mega(t_hbm,o_hbm,p_hbm,ax_hbm,ay_hbm,wz_hbm,q_hbm,out,tc,ec,t_ref,vp,ax_ref,ay_ref,wz_ref,q_ref,xh,xl,part,gs,parts,sums,ub,ub2,ob,sb,kt,e,osend,arecv,brecv,crecv,drecv,tsend,trecv,esend,erecv,loc,tabs,rsend,rrecv,gsend,grecv,usend,urecv,ksem):
     g=lax.axis_index("grp"); o=lax.axis_index("orb"); me=g*64+o
     s=2*lax.rem(o,2)-1
     w=lambda v: lax.rem(v+128,64)
@@ -245,21 +245,24 @@
     mid(2)
     mid(3)
     mid(4)
-    def e_send(k,c):
-        d=lax.rem(k,2)*64+lax.div(k,2)
+    def e_send(q,k,c):
+        n=q*4*CP+lax.rem(k+5*me,4*CP)
+        d=lax.rem(n,2)*64+lax.div(n,2)
         src=piece(e,d)
         @pl.when(d==me)
         def _(): pltpu.make_async_copy(src,ec.at[mine,:],erecv).start()
         @pl.when(d!=me)
         def _(): pltpu.make_async_remote_copy(src_ref=src,dst_ref=ec.at[mine,:],send_sem=esend,recv_sem=erecv,device_id=peer(d),device_id_type=MESH).start()
         return c
-    def tail(q):
+    def tail(i):
+        q=lax.rem(i+lax.div(o,2),CH)
         inv([2,3,4],q,False)
-        lax.fori_loop(q*4*CP,(q+1)*4*CP,e_send,0)
+        lax.fori_loop(0,4*CP,functools.partial(e_send,q),0)
     chunks(tail)
     whole=lambda buf,n,sem: pltpu.make_async_copy(buf.at[pl.ds(0,n),:],buf.at[pl.ds(0,n),:],sem).wait()
     def spread(lo,hi):
-        def send(n,c):
+        def send(k,c):
+            n=lo+lax.rem(k+me,hi-lo)
             src=part.at[pl.ds(pl.multiple_of(n*8,8),8),:]
             h=home(n)
             @pl.when(h==me)
@@ -267,7 +270,7 @@
             @pl.when(h!=me)
             def _(): pltpu.make_async_remote_copy(src_ref=src,dst_ref=parts.at[me],send_sem=rsend,recv_sem=rrecv,device_id=peer(h),device_id_type=MESH).start()
             return c
-        lax.fori_loop(lo,hi,send,0)
+        lax.fori_loop(0,hi-lo,send,0)
     def nt(a,b): return lax.dot_general(a,b,(((1,),(1,)),((),())),preferred_element_type=F32)
     def rowset(buf,s): return buf[pl.ds(s,128,stride=16),:]
     def vrow(s): return vp[pl.ds(g*16+s,1),:]
@@ -283,35 +286,47 @@
     for s in range(16):
         h,l=split(rowset(ec,s))
         xh[0:128,128*s:128*s+128]=h; xl[0:128,128*s:128*s+128]=l
-    part[0:256,:]=(nt(xh[...],xh[0:128,:])+nt(xh[...],xl[0:128,:])+nt(xl[...],xh[0:128,:]))*(1.0/CELLS)
-    spread(0,32)
+    def gram_rows(a):
+        part[a:a+128,:]=(nt(xh[a:a+128,:],xh[0:128,:])+nt(xh[a:a+128,:],xl[0:128,:])+nt(xl[a:a+128,:],xh[0:128,:]))*(1.0/CELLS)
+    gram_rows(0)
+    spread(0,16)
+    gram_rows(128)
+    spread(16,32)
+    line=[lax.rem(lax.div(o,2)+dx,4)*2+lax.rem(o+dc,2) for dx in (2,3,1,0) for dc in (1,0)]
     def gather(n,c):
         @pl.when(home(n)==me)
         def _():
             pltpu.make_async_copy(parts,parts,rrecv).wait()
             sums[...]=jnp.sum(parts[...],axis=0)
             dst=gs.at[pl.ds(pl.multiple_of(n*8,8),8),:]
-            pltpu.make_async_copy(sums,dst,grecv).start()
+            late=(n>=16).astype(jnp.int32)
+            pltpu.make_async_copy(sums,dst,grecv.at[late]).start()
             def bc(j,c2):
                 step=lambda v: jnp.where(v<2,2+v,3-v)
-                dz,dy,dx=step(lax.div(j,32)),step(lax.rem(lax.div(j,8),4)),step(lax.rem(lax.div(j,2),4))
-                y=lax.rem(2*lax.div(o,32)+g+dy,4)
-                z=lax.rem(lax.div(o,8)+dz,4)
-                x=lax.rem(lax.div(o,2)+dx,4)
-                c=lax.rem(o+1+j,2)
-                pltpu.make_async_remote_copy(src_ref=sums,dst_ref=dst,send_sem=gsend,recv_sem=grecv,device_id=(lax.rem(y,2),lax.div(y,2)*32+z*8+x*2+c),device_id_type=MESH).start()
+                y=lax.rem(2*lax.div(o,32)+g+step(lax.rem(j,4)),4)
+                z=lax.rem(lax.div(o,8)+step(lax.div(j,4)),4)
+                row,base=lax.rem(y,2),lax.div(y,2)*32+z*8
+                def go(v): pltpu.make_async_remote_copy(src_ref=sums,dst_ref=dst,send_sem=gsend,recv_sem=grecv.at[late],device_id=(row,base+v),device_id_type=MESH).start()
+                for v in line[:-1]: go(v)
+                @pl.when(j<15)
+                def _(): go(line[-1])
                 return c2
-            lax.fori_loop(0,NDEV-1,bc,0)
+            lax.fori_loop(0,16,bc,0)
         return c
     lax.fori_loop(0,48,gather,0)
-    pltpu.make_async_copy(gs,gs,grecv).wait()
+    def summed(a,b,i): pltpu.make_async_copy(gs.at[a:b,:],gs.at[a:b,:],grecv.at[i]).wait()
+    summed(0,128,0)
     HI=lax.Precision.HIGHEST
     def solve_small():
+        sb[0,256:384,:]=spd_inverse(gs[0:128,:])
+    def combine():
         gte=gs[128:256,:]
-        m=jnp.dot(gte,spd_inverse(gs[0:128,:]),precision=HI,preferred_element_type=F32)
+        m=jnp.dot(gte,sb[0,256:384,:],precision=HI,preferred_element_type=F32)
         sb[0,0:128,:]=m
         sb[0,128:256,:]=gs[256:384,:]-lax.dot_general(m,gte,(((1,),(1,)),((),())),precision=HI,preferred_element_type=F32)
     loop(0,1+lax.div(o,64),lambda i: solve_small())
+    summed(128,384,1)
+    loop(0,1+lax.div(o,64),lambda i: combine())
     def coeff(which):
         b=which*64
         h0,l0=split(sb[0,pl.ds(pl.multiple_of(b,64),64),:]); h1,l1=split(sb[0,pl.ds(pl.multiple_of(128+b,64),64),:])
@@ -331,7 +346,10 @@
         ub[:,part_of(0,i)]=rows_of(other,i)
         swap_copy(i).start()
     loop(0,16//N,theirs)
-    def ours(i): out[:,part_of(g*2048,i)]=rows_of(g,i)
+    def keep(i): return pltpu.make_async_copy(ub2.at[:,part_of(0,i)],out.at[:,part_of(g*2048,i)],ksem.at[i])
+    def ours(i):
+        ub2[:,part_of(0,i)]=rows_of(g,i)
+        keep(i).start()
     loop(0,16//N,ours)
     def drain(n,c):
         @pl.when(home(n)!=me)
@@ -345,6 +363,7 @@
         pltpu.make_async_copy(ob.at[0,rows(0),:],ob.at[0,rows(0),:],osend).wait()
         return c
     lax.fori_loop(0,16+on_out+on_across-2*single,drain_occ,0)
+    for i in range(16//N): keep(i).wait()
     for i in range(16//N): swap_copy(i).wait()
 
 VM=pl.BlockSpec(memory_space=pltpu.VMEM)
@@ -353,10 +372,10 @@
     tabs=[jnp.asarray(a) for a in tables()]
     D=pltpu.SemaphoreType.DMA
     big=lambda *n: pltpu.VMEM(n+(2048,128),F32)
-    return pl.pallas_call(mega,out_shape=jax.ShapeDtypeStruct((64,4096),F32),in_specs=[ANY]*7,out_specs=VM,
+    return pl.pallas_call(mega,out_shape=jax.ShapeDtypeStruct((64,4096),F32),in_specs=[ANY]*7,out_specs=ANY,
       scratch_shapes=[big(),big(),big(),pltpu.VMEM((32,128),F32),pltpu.VMEM((64,192),BF),pltpu.VMEM((64,192),BF),pltpu.VMEM((256,256),BF),pltpu.VMEM((96,128),F32),
-        pltpu.VMEM((256,2048),BF),pltpu.VMEM((256,2048),BF),pltpu.VMEM((384,128),F32),pltpu.VMEM((384,128),F32),pltpu.VMEM((128,8,128),F32),pltpu.VMEM((8,128),F32),pltpu.VMEM((64,2048),F32),
-        big(5),big(5),big(),big(),D,D((CH,)),D((CH,)),D((CH,)),D((CH,)),D,D,D,D,D,D((7,)),D,D,D,D,D((4,)),D((4,))],
+        pltpu.VMEM((256,2048),BF),pltpu.VMEM((256,2048),BF),pltpu.VMEM((384,128),F32),pltpu.VMEM((384,128),F32),pltpu.VMEM((128,8,128),F32),pltpu.VMEM((8,128),F32),pltpu.VMEM((64,2048),F32),pltpu.VMEM((64,2048),F32),
+        big(5),big(5),big(),big(),D,D((CH,)),D((CH,)),D((CH,)),D((CH,)),D,D,D,D,D,D((7,)),D,D,D,D((2,)),D((4,)),D((4,)),D((4,))],
       compiler_params=pltpu.CompilerParams(collective_id=0,has_side_effects=True,vmem_limit_bytes=58<<20))(t,o,p,*tabs)
 
 def on_device(occupied, targets, potential):

time: 104 us -> 98.9 us (0.951)
  Pallas kernels: 102 us -> 96.5 us
    pallas_call x1, Pallas kernels: 102 us -> 96.5 us  [mega_call(): pl.pallas_call(mega, out_shape=jax.ShapeDtypeStruct((64, 4096), F32), in_...]
where the time goes in v4:
time: 98.9 us; the launch traced here: 98.8 us
  Pallas kernels  96.5 us (98%)
  local copies, waits for them, and re-layouts  2.27 us (2%)
    pallas_call x1, Pallas kernels, mega_call(): pl.pallas_call(mega, out_shape=jax.ShapeDtypeStruct((64, 4096), F32), in_...  96.5 us
    unnamed x1, local copies, waits for them, and re-layouts  2.27 us

profile of v4, /device:TPU:1, one launch (start us, length us, event | category | flops | bytes accessed | tf_op | source)
XLA Modules:
  0.0 98.8 jit_solution(10371114956145722692)
XLA Ops:
  0.0 96.5 %shard_map.73 = f32[64,4096]{1,0:T(8,128)} custom-call(f32[2048,128]{1,0:T(8,128)} %bitcast.3, f32[2048,128]{1,0:T(8,128)} %bitcast.4, f32[32,128]{1,0:T(8,128)} %bitcast.5, bf16[64,192]{1,0:T(8,128)(2,1)} %constant.8.clone.ax_hbm, bf16[64,192]{1,0:T(8,128)(2,1)} %constant.9.clone.ay_hbm, bf16[256,256]{1,0:T(8,128)(2,1)} %constant.10.clone.wz_hbm, ...), custom_call_target="tpu_custom_call" | custom-call | tf_op jit(solution)/shard_map/pallas_call | solution.py:375
  96.5 2.3 %copy.9 = f32[64,4096]{1,0:T(8,128)} copy(f32[64,4096]{1,0:T(8,128)} %shard_map.73) | data formatting | bytes 2097152
